TPU v7x, 32 devices: a whole 2x2x4 slice. The times are simulated.
32 devices in a mesh: dp: 8 (over y, x, core), seq: 4 (over z).
Axes of the slice: x: 2, y: 2, z: 4, core: 2. Of those that a mesh axis runs over, the one named last changes fastest.
Arguments:
- tokens: int32 [8, 1024], P('dp', 'seq'), may hold values from 0 to 3
- embedding: float32 [4, 384], replicated, may hold values from -6 to 6
- gain_in: float32 [384], replicated, may hold values from 0.5 to 1.5
- conv_taps: float32 [384, 4], replicated, may hold values from -3 to 3
- long_filter: float32 [384, 1024], P('seq'), may hold values from -6 to 6
- gain_mid: float32 [384], replicated, may hold values from 0.5 to 1.5
- mlp_weights: bfloat16 [2304, 384], replicated, may hold values from -0.3125 to 0.3125
- cotangent: bfloat16 [8, 768, 1024], P('dp', None, 'seq'), may hold values from -6 to 6
Outputs:
- layer_out: bfloat16 [8, 768, 1024], P('dp', None, 'seq')
- grad_embedding: float32 [4, 384], replicated
- grad_gain_in: float32 [384], replicated
- grad_conv: float32 [384, 4], replicated
- grad_filter: float32 [384, 1024], P('seq')
- grad_gain_mid: float32 [384], replicated
- grad_mlp: float32 [2304, 384], P('dp', 'seq')
All inputs are finite; a program needn't handle non-finite values.
Results may differ from a plain program's by a relative error of at most 0.03.
Values may be sent and summed in bfloat16 or wider, within the bound.
A program may use at most 64 MiB of HBM per device.

v0:
```python
import jax
import jax.numpy as jnp
import numpy as np
from jax import lax
from jax.sharding import PartitionSpec as P

F32 = jnp.float32
BF16 = jnp.bfloat16


def dct_table(length):
    freq = np.arange(length)[:, None]
    place = np.arange(length)[None, :]
    phase = (2 * place + 1) * freq % (4 * length)
    weight = np.where(freq == 0, np.sqrt(1.0 / length), np.sqrt(2.0 / length))
    return (weight * np.cos(np.pi * phase / (2 * length))).astype(np.float32).astype(BF16)


def dot(a, b, dims):
    return lax.dot_general(a, b, (dims, ((), ())), preferred_element_type=F32)


def compute(ids_block, ids_own, q_rows, q_own, embedding, gain_in, conv_taps, filt, gain_mid, mlp, cot):
    taps = conv_taps.shape[1]
    channels = embedding.shape[1]
    block_len = q_rows.shape[0]
    hidden = mlp.shape[0] // 3
    local_len = ids_own.shape[0]
    base_scale = lax.rsqrt(jnp.mean(embedding * embedding, axis=1, keepdims=True) + 1e-6)
    base_norm = (embedding * base_scale * gain_in[None, :]).astype(BF16)
    kmer = (conv_taps[:, :, None] * base_norm.astype(F32).T[:, None, :]).reshape(channels, -1).astype(BF16)
    bases = jnp.arange(4, dtype=jnp.int32)[:, None]
    rim = taps - 1
    fwd = [ids_block[rim - k : rim - k + block_len] for k in range(taps)]
    rev = [3 - ids_block[rim + k : rim + k + block_len] for k in range(taps)]
    hot = jnp.concatenate([(row[None, :] == bases) for row in fwd + rev], 0).astype(BF16)
    hot_spec = dot(hot, q_rows, ((1,), (1,))).astype(BF16)
    half = 4 * taps
    specs = [dot(kmer, hot_spec[s * half : (s + 1) * half], ((1,), (0,))).astype(BF16) for s in range(2)]
    scaled = [(filt * spec.astype(F32)).astype(BF16) for spec in specs]
    filtered = jnp.concatenate([dot(one, q_own, ((1,), (0,))) for one in scaled], 1)
    both = jnp.concatenate([ids_own, 3 - ids_own])
    emb_cols = embedding.T
    residual = jnp.zeros((channels, 2 * local_len), F32)
    for a in range(4):
        residual = residual + jnp.where(both[None, :] == a, emb_cols[:, a : a + 1], 0.0)
    level = residual + filtered
    mid_scale = lax.rsqrt(jnp.mean(level * level, axis=0, keepdims=True) + 1e-6)
    unit = level * mid_scale
    normed = (unit * gain_mid[:, None]).astype(BF16)
    w_in, w_down = mlp[: 2 * hidden], mlp[2 * hidden :]
    proj = dot(w_in, normed, ((1,), (0,))).astype(BF16).astype(F32)
    gate, up = proj[:hidden], proj[hidden:]
    sig = jax.nn.sigmoid(gate)
    act = (gate * sig * up).astype(BF16)
    combined = (level + dot(w_down, act, ((0,), (0,)))).astype(BF16)
    layer_out = jnp.concatenate([combined[:, :local_len], jnp.flip(combined[:, local_len:], 0)], 0)
    back = jnp.concatenate([cot[:channels], jnp.flip(cot[channels:], 0)], 1)
    d_act = dot(w_down, back, ((1,), (0,)))
    d_gate = d_act * up * sig * (1.0 + gate * (1.0 - sig))
    d_up = d_act * gate * sig
    d_proj = jnp.concatenate([d_gate, d_up], 0).astype(BF16)
    d_normed = dot(w_in, d_proj, ((0,), (0,)))
    grad_in = dot(d_proj, normed, ((1,), (1,)))
    grad_down = dot(act, back, ((1,), (1,)))
    grad_mlp = jnp.concatenate([grad_in, grad_down], 0)
    grad_mid = jnp.sum(d_normed * unit, axis=1, keepdims=True)
    d_unit = d_normed * gain_mid[:, None]
    d_level = back.astype(F32) + mid_scale * (d_unit - unit * jnp.mean(d_unit * unit, axis=0, keepdims=True))
    d_bf = d_level.astype(BF16)
    own_hot = (both[None, :] == bases).astype(BF16)
    d_low = (d_level - d_bf.astype(F32)).astype(BF16)
    base_sum = dot(d_bf, own_hot, ((1,), (1,))) + dot(d_low, own_hot, ((1,), (1,)))
    grad_filter = jnp.zeros(filt.shape, F32)
    kmer_sum = jnp.zeros((channels, half), F32)
    for s in range(2):
        d_scaled = dot(d_bf[:, s * local_len : (s + 1) * local_len], q_own, ((1,), (1,)))
        grad_filter = grad_filter + d_scaled * specs[s].astype(F32)
        d_spec = (filt * d_scaled).astype(BF16)
        kmer_sum = kmer_sum + dot(d_spec, hot_spec[s * half : (s + 1) * half], ((1,), (1,)))
    small = jnp.concatenate([base_sum, kmer_sum, grad_mid], 1)
    return layer_out, grad_mlp, grad_filter, small


def finish(small, embedding, gain_in, conv_taps):
    taps = conv_taps.shape[1]
    channels = embedding.shape[1]
    base_sum = small[:, :4].T
    kmer_sum = small[:, 4 : 4 + 4 * taps].reshape(channels, taps, 4)
    grad_mid = small[:, 4 + 4 * taps]
    base_scale = lax.rsqrt(jnp.mean(embedding * embedding, axis=1, keepdims=True) + 1e-6)
    unit = embedding * base_scale
    base_norm = (unit * gain_in[None, :]).astype(BF16).astype(F32)
    grad_conv = jnp.sum(kmer_sum * base_norm.T[:, None, :], axis=2)
    d_norm = jnp.sum(kmer_sum * conv_taps[:, :, None], axis=1).T
    grad_gain = jnp.sum(d_norm * unit, axis=0)
    d_unit = d_norm * gain_in[None, :]
    grad_emb = base_sum + base_scale * (d_unit - unit * jnp.mean(d_unit * unit, axis=1, keepdims=True))
    return grad_emb, grad_gain, grad_conv, grad_mid


def on_device(tokens, embedding, gain_in, conv_taps, long_filter, gain_mid, mlp_weights, cotangent):
    local_len = tokens.shape[1]
    block_len = long_filter.shape[1]
    rim = conv_taps.shape[1] - 1
    place = lax.axis_index("seq") * local_len
    block_start = place // block_len * block_len
    table = jnp.asarray(dct_table(block_len))
    q_own = lax.dynamic_slice(table, (0, place - block_start), (block_len, local_len))
    all_ids = lax.all_gather(tokens[0], "seq", axis=0, tiled=True)
    filt = lax.all_gather(long_filter.astype(BF16), "seq", axis=0, tiled=True).astype(F32)
    padded = jnp.pad(all_ids, (rim, rim), constant_values=4)
    ids_block = lax.dynamic_slice(padded, (block_start,), (block_len + 2 * rim,))
    layer_out, grad_mlp, grad_filter, small = compute(
        ids_block, tokens[0], table, q_own, embedding, gain_in, conv_taps, filt, gain_mid, mlp_weights, cotangent[0]
    )
    small = lax.psum(small, ("dp", "seq"))
    grad_emb, grad_gain, grad_conv, grad_mid = finish(small, embedding, gain_in, conv_taps)
    mine = lax.psum_scatter(grad_filter.astype(BF16), "seq", scatter_dimension=0, tiled=True)
    filter_out = lax.psum(mine, "dp").astype(F32)
    cols = lax.psum_scatter(grad_mlp.astype(BF16), "seq", scatter_dimension=1, tiled=True).astype(F32)
    mlp_out = lax.psum_scatter(cols, "dp", scatter_dimension=0, tiled=True)
    return layer_out[None], grad_emb, grad_gain, grad_conv, filter_out, grad_mid, mlp_out


def solution(mesh):
    placed = (P("dp", "seq"), P(), P(), P(), P("seq", None), P(), P(), P("dp", None, "seq"))
    return jax.shard_map(
        on_device,
        mesh=mesh,
        in_specs=placed,
        out_specs=(P("dp", None, "seq"), P(), P(), P(), P("seq", None), P(), P("dp", "seq")),
        check_vma=False,
    )
```

profile of v0, /device:TPU:25, one launch (start us, length us, event | category | flops | bytes accessed | tf_op | source)
XLA Modules:
  0.0 225.3 jit_solution(804756925329189845)
XLA Ops:
  7.9 5.8 %all-gather = s32[1,1024]{1,0:T(1,128)S(1)} all-gather(s32[1,256]{1,0:T(1,128)} %param.9), channel_id=2, replica_groups=mesh['dp'=8,'seq'=4] {'seq'}, dimensions={1}, use_global_device_ids=true | all-gather | bytes 5120 | tf_op jit(solution)/shard_map/all_gather | solution.py:110
  17.1 2.4 %convolution_convert_fusion.5 = bf16[32,1024]{1,0:T(8,128)(2,1)S(1)} fusion(pred[32,1024]{1,0:T(32,128)(4,1)S(1)} %concatenate.51, bf16[1024,1024]{1,0:T(8,128)(2,1)} %constant.51.clone), kind=kOutput, calls=%fused_computation.33 | convolution fusion | flops 67141632 | bytes 2195456 | tf_op jit(solution)/shard_map/dot_general | solution.py:20
  19.5 1.3 convolution_convert_fusion.2
  20.8 1.3 convolution_convert_fusion.3
  23.8 2.2 rev.8
  26.0 15.2 %all_gather.6 = bf16[384,1024]{1,0:T(8,128)(2,1)S(1)} all-gather(bf16[96,1024]{1,0:T(8,128)(2,1)S(1)} %convert_element_type.91), channel_id=1, replica_groups=mesh['dp'=8,'seq'=4] {'seq'}, dimensions={0}, use_global_device_ids=true | all-gather | bytes 983040 | tf_op jit(solution)/shard_map/all_gather | solution.py:111
  41.2 1.7 fusion.17
  45.6 2.0 fusion.8
  47.5 1.6 multiply_reduce_fusion.1
  51.7 2.0 fusion.1
  53.7 1.9 convolution_convert_fusion.4
  55.7 1.8 convolution_convert_fusion.1
  57.5 1.4 pad_maximum_fusion
  58.8 3.9 %copy.25 = bf16[2304,384]{0,1:T(8,128)(2,1)} copy(bf16[2304,384]{1,0:T(8,128)(2,1)} %pad_maximum_fusion) | data formatting | bytes 3538944
  62.8 1.9 fusion.12
  67.5 2.3 %fusion.24 = f32[384,16]{0,1:T(8,128)} fusion(f32[384,1024]{1,0:T(8,128)} %get-tuple-element.55, bf16[384,1024]{1,0:T(8,128)(2,1)S(1)} %all_gather.6, bf16[32,1024]{1,0:T(8,128)(2,1)S(1)} %copy-done.9), kind=kOutput, calls=%fused_computation.46 | convolution fusion | flops 13762560 | bytes 2416640 | tf_op jit(solution)/shard_map/dot_general | solution.py:20
  69.9 10.6 %reduce-scatter.6.cloned.1.call-done = bf16[96,1024]{1,0:T(8,128)(2,1)} async-done(((bf16[384,1024]{1,0:T(8,128)(2,1)}), bf16[96,1024]{1,0:T(8,128)(2,1)}) %reduce-scatter.6.cloned.1.call-update) | async-done | bytes 196624 | tf_op jit(solution)/shard_map/reduce_scatter | solution.py:119
  82.8 38.7 %reduce-scatter.10.cloned.1.call-done = bf16[96,2304]{1,0:T(8,128)(2,1)} async-done(((bf16[384,2304]{1,0:T(8,128)(2,1)}), bf16[96,2304]{1,0:T(8,128)(2,1)}) %reduce-scatter.10.cloned.1.call-update) | async-done | bytes 442384
  121.4 2.1 copy.26
  123.5 2.2 convert_element_type.117
  127.9 39.8 %psum.14 = f32[384,21]{0,1:T(8,128)S(1)} all-reduce(f32[384,21]{0,1:T(8,128)S(1)} %pad_maximum_fusion.7), channel_id=1, replica_groups=mesh['dp'=8,'seq'=4] {'dp','seq'}, use_global_device_ids=true, to_apply=%region_4.5 | all-reduce | flops 8064 | bytes 64512 | tf_op jit(solution)/shard_map/psum | solution.py:117
  170.3 8.3 %all-reduce.3.cloned.1.call-done = bf16[96,1024]{1,0:T(8,128)(2,1)} async-done(((bf16[96,1024]{1,0:T(8,128)(2,1)}), bf16[96,1024]{1,0:T(8,128)(2,1)}) %all-reduce.3.cloned.1.call-update) | async-done | bytes 196624 | tf_op jit(solution)/shard_map/psum | solution.py:120
  178.5 1.7 convert_element_type.116
  180.2 38.6 %reduce-scatter.8.cloned.1.call-done = f32[288,96]{1,0:T(8,128)} async-done(((f32[2304,96]{1,0:T(8,128)}), f32[288,96]{1,0:T(8,128)}) %reduce-scatter.8.cloned.1.call-update) | async-done | bytes 110608 | tf_op jit(solution)/shard_map/reduce_scatter | solution.py:122
  (111 shorter events, 20.6 us)
Async XLA Ops:
  7.2 73.3 %reduce-scatter.6.cloned.1.call-start = ((), (), s32[]{:S(2)}) async-start(), calls=%async_computation.3 | async-start | bytes 983040 | tf_op jit(solution)/shard_map/reduce_scatter | solution.py:119
  17.1 5.0 %copy-start.12 = (f32[4,384]{1,0:T(4,128)S(1)}, f32[4,384]{1,0:T(4,128)}, u32[]{:S(2)}) copy-start(f32[4,384]{1,0:T(4,128)} %param.10) | copy-start | bytes 18436
  17.1 5.6 %copy-start.10 = (f32[96,1024]{1,0:T(8,128)S(1)}, f32[96,1024]{1,0:T(8,128)}, u32[]{:S(2)}) copy-start(f32[96,1024]{1,0:T(8,128)} %param.13) | copy-start | bytes 1179652
  19.5 3.2 %copy-start.8 = (bf16[32,1024]{1,0:T(8,128)(2,1)}, bf16[32,1024]{1,0:T(8,128)(2,1)S(1)}, u32[]{:S(2)}) copy-start(bf16[32,1024]{1,0:T(8,128)(2,1)S(1)} %convolution_convert_fusion.5) | copy-start | bytes 196612
  19.5 3.2 %copy-start.11 = (bf16[1,768,256]{2,1,0:T(8,128)(2,1)S(1)}, bf16[1,768,256]{2,1,0:T(8,128)(2,1)}, u32[]{:S(2)}) copy-start(bf16[1,768,256]{2,1,0:T(8,128)(2,1)} %param.16) | copy-start | bytes 1179652
  22.8 18.4 %copy-start = (bf16[1024,1024]{1,0:T(8,128)(2,1)S(1)}, bf16[1024,1024]{1,0:T(8,128)(2,1)}, u32[]{:S(2)}) copy-start(bf16[1024,1024]{1,0:T(8,128)(2,1)} %constant.51.clone) | copy-start | bytes 6291460
  41.2 1.7 copy-start.3
  43.0 1.5 copy-start.5
  44.1 5.0 %copy-start.17 = (f32[512]{0:T(512)}, f32[512]{0:T(512)S(1)}, u32[]{:S(2)}) copy-start(f32[512]{0:T(512)S(1)} %add_rsqrt_fusion) | copy-start | bytes 6148
  47.5 1.6 copy-start.26
  47.5 1.6 copy-start.28
  49.1 1.9 copy-start.1
  53.6 67.8 %reduce-scatter.10.cloned.1.call-start = ((), (), s32[]{:S(2)}) async-start(), calls=%async_computation.6 | async-start | bytes 2211840
  53.7 2.0 copy-start.27
  53.7 2.0 copy-start.29
  62.7 115.8 %all-reduce.3.cloned.1.call-start = ((), (), s32[]{:S(2)}) async-start(), calls=%async_computation.4 | async-start | bytes 393216 | tf_op jit(solution)/shard_map/psum | solution.py:120
  64.7 2.9 %copy-start.9 = (bf16[32,1024]{1,0:T(8,128)(2,1)S(1)}, bf16[32,1024]{1,0:T(8,128)(2,1)}, u32[]{:S(2)}) copy-start(bf16[32,1024]{1,0:T(8,128)(2,1)} %copy-done.8) | copy-start | bytes 196612
  66.7 13.8 %copy-start.15 = (s32[512]{0:T(512)}, s32[512]{0:T(512)S(1)}, u32[]{:S(2)}) copy-start(s32[512]{0:T(512)S(1)} %pad_add_fusion) | copy-start | bytes 6148
  80.5 138.3 %reduce-scatter.8.cloned.1.call-start = ((), (), s32[]{:S(2)}) async-start(), calls=%async_computation.5 | async-start | bytes 1327104 | tf_op jit(solution)/shard_map/reduce_scatter | solution.py:122
  123.5 2.3 %copy-start.4 = (f32[384,512]{0,1:T(8,128)S(1)}, f32[384,512]{0,1:T(8,128)}, u32[]{:S(2)}) copy-start(f32[384,512]{0,1:T(8,128)} %get-tuple-element.32) | copy-start | bytes 2359300
  125.8 2.0 copy-start.23
  126.7 41.6 %copy-start.14 = (f32[384,4]{0,1:T(4,128)S(1)}, f32[384,4]{0,1:T(4,128)}, u32[]{:S(2)}) copy-start(f32[384,4]{0,1:T(4,128)} %param.12) | copy-start | bytes 18436
  126.7 42.2 %copy-start.16 = (f32[384]{0:T(512)S(1)}, f32[384]{0:T(512)}, u32[]{:S(2)}) copy-start(f32[384]{0:T(512)} %param.11) | copy-start | bytes 4612
  126.7 42.2 %copy-start.25 = (f32[4]{0:T(128)S(1)}, f32[4]{0:T(128)}, u32[]{:S(2)}) copy-start(f32[4]{0:T(128)} %copy-done.24) | copy-start | bytes 52
  (10 other events, 9.8 us)
Sparse Core Ops, SparseCore 0:
  53.8 26.6 reduce-scatter.5
  82.8 38.5 reduce-scatter.9
  124.5 53.9 all-reduce.2
  182.2 36.5 reduce-scatter.7
where the time goes:
time: 228 us; the launch traced here: 225 us
  waiting for transfers between devices  96.2 us (42%)
  blocking collectives  60.8 us (27%)
  matrix products  24.8 us (11%)
  local copies, waits for them, and re-layouts  15.6 us (7%)
  between operations  14.2 us (6%)
  other arithmetic  13.5 us (6%)
    psum x1, blocking collectives, on_device(): small = lax.psum(small, ('dp', 'seq'))  39.8 us
    unnamed x5, waiting for transfers between devices  38.7 us
    reduce_scatter x1, waiting for transfers between devices, on_device(): mlp_out = lax.psum_scatter(cols, 'dp', scatter_dimension=0, tiled=True)  38.6 us
    dot_general x17, matrix products, dot(): return lax.dot_general(a, b, (dims, ((), ())), preferred_element_type=F32)  24.8 us
    all_gather x1, blocking collectives, on_device(): lax.all_gather(long_filter.astype(BF16), 'seq', axis=0, tiled=True)  15.2 us
    reduce_scatter x1, waiting for transfers between devices, on_device(): lax.psum_scatter(grad_filter.astype(BF16), 'seq', scatter_dimension=0, ti...  10.6 us
    unnamed x65, local copies, waits for them, and re-layouts  9.33 us
    psum x1, waiting for transfers between devices, on_device(): filter_out = lax.psum(mine, 'dp').astype(F32)  8.27 us
  transfers between devices with their start and end apart: 4, of which 4 were waited for; matrix products, arithmetic and copies ran while one was open for 13% of the time, Pallas kernels for 0%

commit v1 on v0

--- a/solution.py
+++ b/solution.py
@@ -2,6 +2,8 @@
 import jax.numpy as jnp
 import numpy as np
 from jax import lax
+from jax.experimental import pallas as pl
+from jax.experimental.pallas import tpu as pltpu
 from jax.sharding import PartitionSpec as P
 
 F32 = jnp.float32
@@ -78,7 +80,7 @@
         grad_filter = grad_filter + d_scaled * specs[s].astype(F32)
         d_spec = (filt * d_scaled).astype(BF16)
         kmer_sum = kmer_sum + dot(d_spec, hot_spec[s * half : (s + 1) * half], ((1,), (1,)))
-    small = jnp.concatenate([base_sum, kmer_sum, grad_mid], 1)
+    small = jnp.concatenate([base_sum, kmer_sum, grad_mid], 1).T
     return layer_out, grad_mlp, grad_filter, small
 
 
@@ -99,6 +101,241 @@
     return grad_emb, grad_gain, grad_conv, grad_mid
 
 
+MESH = pl.DeviceIdType.MESH
+
+
+def greet(dp_peers, seq_peers):
+    barrier = pltpu.get_barrier_semaphore()
+    for peer in dp_peers:
+        pl.semaphore_signal(barrier, inc=1, device_id=peer, device_id_type=MESH)
+    for peer in seq_peers:
+        pl.semaphore_signal(barrier, inc=1, device_id=peer, device_id_type=MESH)
+    pl.semaphore_wait(barrier, len(dp_peers) + len(seq_peers))
+
+
+def remote(src, dst, send, recv, peer):
+    return pltpu.make_async_remote_copy(
+        src_ref=src, dst_ref=dst, send_sem=send, recv_sem=recv, device_id=peer, device_id_type=MESH
+    )
+
+
+def ring_of(at, count, spot):
+    return [spot(lax.rem(at + off, count)) for off in range(1, count)]
+
+
+def gather_kernel(n_seq, shard, ids, gath, all_ids, send, recv, swap_send, swap_recv, id_send, id_recv):
+    dp, sq = lax.axis_index("dp"), lax.axis_index("seq")
+    core = lax.rem(dp, 2)
+    mate = (dp + 1 - 2 * core, sq)
+    peers = ring_of(sq, n_seq, lambda j: (dp, j))
+    greet([mate], peers)
+    sends = []
+    for off in range(1, n_seq):
+        id_copy = remote(ids, all_ids.at[sq], id_send.at[off], id_recv.at[off], peers[off - 1])
+        copy = remote(shard.at[core], gath.at[sq, core], send.at[off], recv.at[off], peers[off - 1])
+        id_copy.start()
+        copy.start()
+        sends += [id_copy, copy]
+    all_ids[sq] = ids[...]
+    gath[sq] = shard[...]
+    for off in [*range(n_seq - 1, 0, -1)]:
+        source = lax.rem(sq - off + n_seq, n_seq)
+        landed = gath.at[source, core]
+        remote(landed, landed, send.at[off], recv.at[off], mate).wait_recv()
+        swap = remote(landed, landed, swap_send.at[off], swap_recv.at[off], mate)
+        swap.start()
+        sends.append(swap)
+    for off in range(1, n_seq):
+        source = lax.rem(sq - off + n_seq, n_seq)
+        other = gath.at[source, 1 - core]
+        remote(other, other, swap_send.at[off], swap_recv.at[off], mate).wait_recv()
+        got = all_ids.at[source]
+        remote(got, got, id_send.at[off], id_recv.at[off], mate).wait_recv()
+    for copy in sends:
+        copy.wait_send()
+
+
+def gather_all(n_seq, shard, ids):
+    rows, width = shard.shape
+    halves = shard.reshape(2, rows // 2, width)
+    vmem = pl.BlockSpec(memory_space=pltpu.VMEM)
+    dma = pltpu.SemaphoreType.DMA((n_seq,))
+    gath, all_ids = pl.pallas_call(
+        lambda *refs: gather_kernel(n_seq, *refs),
+        out_shape=(
+            jax.ShapeDtypeStruct((n_seq,) + halves.shape, shard.dtype),
+            jax.ShapeDtypeStruct((n_seq,) + ids.shape, ids.dtype),
+        ),
+        in_specs=[vmem] * 2,
+        out_specs=[vmem] * 2,
+        scratch_shapes=[dma] * 6,
+        compiler_params=pltpu.CompilerParams(collective_id=0, has_side_effects=True),
+        name="gather",
+    )(halves, ids)
+    return gath.reshape(n_seq * rows, width), all_ids.reshape(-1)
+
+
+def at_axis(axis, index):
+    return (slice(None),) * axis + (index,)
+
+
+def reduce_kernel(n_dp, n_seq, mlp_a, mlp_b, filt, small, mlp_out, filt_out, small_out, *scratch):
+    bits = n_dp.bit_length() - 1
+    stages = bits
+    per = 2 * stages
+    rec_a, rec_b, rec_f = scratch[0:stages], scratch[stages:per], scratch[per : per + stages]
+    rest = scratch[per + stages :]
+    acc_a, acc_b, acc_f = rest[0:stages], rest[stages:per], rest[per : per + stages]
+    small_acc, small_rec, z_mlp, z_mlp_rec, z_f_rec, z_s_rec, mine, gath = rest[per + stages : per + stages + 8]
+    send, recv, z_send, z_recv, g_send, g_recv = rest[per + stages + 8 :]
+    dp, sq = lax.axis_index("dp"), lax.axis_index("seq")
+    dp_peers = ring_of(dp, n_dp, lambda i: (i, sq))
+    seq_peers = ring_of(sq, n_seq, lambda j: (dp, j))
+    greet(dp_peers, seq_peers)
+    order_a = [*range(bits)]
+    order_b = [0] + [*range(2, bits)] + ([1] if bits > 1 else [])
+    left_a = [*range(bits - 1, -1, -1)]
+    left_b = [*range(bits - 1, -1, -1)]
+    cur_a, cur_b, cur_f, cur_s = mlp_a, mlp_b, filt, small
+    waits = []
+    for stage in range(stages):
+        bit_a, bit_b = order_a[stage], order_b[stage]
+        my_a, my_b = lax.rem(dp // 2**bit_a, 2), lax.rem(dp // 2**bit_b, 2)
+        to_a = (dp + (1 - 2 * my_a) * 2**bit_a, sq)
+        to_b = (dp + (1 - 2 * my_b) * 2**bit_b, sq)
+        ax_a, ax_b = left_a.index(bit_a), left_b.index(bit_b)
+        copies = [
+            remote(cur_a.at[at_axis(ax_a, 1 - my_a)], rec_a[stage], send.at[stage, 0], recv.at[stage, 0], to_a),
+            remote(cur_f.at[at_axis(ax_b, 1 - my_b)], rec_f[stage], send.at[stage, 1], recv.at[stage, 1], to_b),
+            remote(cur_b.at[at_axis(ax_b, 1 - my_b)], rec_b[stage], send.at[stage, 2], recv.at[stage, 2], to_b),
+            remote(cur_s, small_rec.at[stage], send.at[stage, 3], recv.at[stage, 3], to_a),
+        ]
+        for copy in copies:
+            copy.start()
+        waits += copies
+        copies[0].wait_recv()
+        acc_a[stage][...] = (cur_a[at_axis(ax_a, my_a)].astype(F32) + rec_a[stage][...].astype(F32)).astype(BF16)
+        copies[1].wait_recv()
+        acc_f[stage][...] = (cur_f[at_axis(ax_b, my_b)].astype(F32) + rec_f[stage][...].astype(F32)).astype(BF16)
+        copies[2].wait_recv()
+        acc_b[stage][...] = (cur_b[at_axis(ax_b, my_b)].astype(F32) + rec_b[stage][...].astype(F32)).astype(BF16)
+        copies[3].wait_recv()
+        small_acc[stage] = cur_s[...] + small_rec[stage]
+        cur_a, cur_b, cur_f, cur_s = acc_a[stage], acc_b[stage], acc_f[stage], small_acc.at[stage]
+        left_a.remove(bit_a)
+        left_b.remove(bit_b)
+    joined = jnp.concatenate([cur_a[...], cur_b[...]], 1)
+    cols = joined.shape[1] // n_seq
+    for j in range(n_seq):
+        z_mlp[j] = joined[:, j * cols : (j + 1) * cols]
+    for off in range(1, n_seq):
+        to = lax.rem(sq + off, n_seq)
+        copies = [
+            remote(cur_f.at[to], z_f_rec.at[off], z_send.at[0, off], z_recv.at[0, off], (dp, to)),
+            remote(cur_s, z_s_rec.at[sq], z_send.at[1, off], z_recv.at[1, off], (dp, to)),
+            remote(z_mlp.at[to], z_mlp_rec.at[off], z_send.at[2, off], z_recv.at[2, off], (dp, to)),
+        ]
+        for copy in copies:
+            copy.start()
+        waits += copies
+    z_s_rec[sq] = cur_s[...]
+    total = cur_f[sq].astype(F32)
+    for off in range(1, n_seq):
+        slot = z_f_rec.at[off]
+        remote(slot, slot, z_send.at[0, off], z_recv.at[0, off], (dp, sq)).wait_recv()
+        total = total + z_f_rec[off].astype(F32)
+    mine[...] = total.astype(BF16)
+    for off in range(1, n_dp):
+        to = lax.rem(dp + off, n_dp)
+        copy = remote(mine, gath.at[dp], g_send.at[off], g_recv.at[off], (to, sq))
+        copy.start()
+        waits.append(copy)
+    gath[dp] = mine[...]
+    for off in range(1, n_seq):
+        source = lax.rem(sq - off + n_seq, n_seq)
+        slot = z_s_rec.at[source]
+        remote(slot, slot, z_send.at[1, off], z_recv.at[1, off], (dp, sq)).wait_recv()
+        slot = z_mlp_rec.at[off]
+        remote(slot, slot, z_send.at[2, off], z_recv.at[2, off], (dp, sq)).wait_recv()
+    total = z_mlp[sq].astype(F32)
+    for off in range(1, n_seq):
+        total = total + z_mlp_rec[off].astype(F32)
+    mlp_out[...] = total
+    total = z_s_rec[0]
+    for j in range(1, n_seq):
+        total = total + z_s_rec[j]
+    small_out[...] = total
+    for off in range(1, n_dp):
+        source = lax.rem(dp - off + n_dp, n_dp)
+        slot = gath.at[source]
+        remote(slot, slot, g_send.at[off], g_recv.at[off], (dp, sq)).wait_recv()
+    filt_out[...] = gath[...].astype(F32)
+    for copy in waits:
+        copy.wait_send()
+
+
+def reduce_all(n_dp, n_seq, grad_mlp, grad_filter, small):
+    bits = n_dp.bit_length() - 1
+    twos = (2,) * bits
+    rows, width = grad_mlp.shape
+    part = rows // n_dp
+    lanes = 128
+    cut = width // lanes * 2 // 3 * lanes
+    mlp = grad_mlp.astype(BF16).reshape(twos + (part, width))
+    mlp_a, mlp_b = mlp[..., :cut], mlp[..., cut:]
+    chan, length = grad_filter.shape
+    own = chan // n_seq
+    tidy = length % (n_dp * lanes) == 0
+    filt = grad_filter.astype(BF16)
+    if tidy:
+        filt = filt.reshape(n_seq, own, n_dp, length // n_dp).transpose(2, 0, 1, 3)
+    else:
+        filt = filt.reshape(n_seq, n_dp, -1, lanes).transpose(1, 0, 2, 3)
+    f_tail = filt.shape[1:]
+    filt = filt.reshape(twos + f_tail)
+
+    def halves(tail):
+        return [pltpu.VMEM(twos[stage + 1 :] + tail, BF16) for stage in range(bits)]
+
+    tails = [(part, cut), (part, width - cut), f_tail]
+    buffers = [b for tail in tails for b in halves(tail)]
+    cols = width // n_seq
+    dma = pltpu.SemaphoreType.DMA
+    vmem = pl.BlockSpec(memory_space=pltpu.VMEM)
+    mlp_out, filt_out, small_out = pl.pallas_call(
+        lambda *refs: reduce_kernel(n_dp, n_seq, *refs),
+        out_shape=(
+            jax.ShapeDtypeStruct((part, cols), F32),
+            jax.ShapeDtypeStruct((n_dp,) + f_tail[1:], F32),
+            jax.ShapeDtypeStruct(small.shape, F32),
+        ),
+        in_specs=[vmem] * 4,
+        out_specs=[vmem] * 3,
+        scratch_shapes=buffers * 2
+        + [
+            pltpu.VMEM((bits,) + small.shape, F32),
+            pltpu.VMEM((bits,) + small.shape, F32),
+            pltpu.VMEM((n_seq, part, cols), BF16),
+            pltpu.VMEM((n_seq, part, cols), BF16),
+            pltpu.VMEM(f_tail, BF16),
+            pltpu.VMEM((n_seq,) + small.shape, F32),
+            pltpu.VMEM(f_tail[1:], BF16),
+            pltpu.VMEM((n_dp,) + f_tail[1:], BF16),
+            dma((bits, 4)),
+            dma((bits, 4)),
+            dma((3, n_seq)),
+            dma((3, n_seq)),
+            dma((n_dp,)),
+            dma((n_dp,)),
+        ],
+        compiler_params=pltpu.CompilerParams(collective_id=1, has_side_effects=True, vmem_limit_bytes=50 * 2**20),
+        name="reduce",
+    )(mlp_a, mlp_b, filt, small)
+    if tidy:
+        filt_out = filt_out.transpose(1, 0, 2)
+    return mlp_out, filt_out.reshape(own, length), small_out
+
+
 def on_device(tokens, embedding, gain_in, conv_taps, long_filter, gain_mid, mlp_weights, cotangent):
     local_len = tokens.shape[1]
     block_len = long_filter.shape[1]
@@ -107,19 +344,16 @@
     block_start = place // block_len * block_len
     table = jnp.asarray(dct_table(block_len))
     q_own = lax.dynamic_slice(table, (0, place - block_start), (block_len, local_len))
-    all_ids = lax.all_gather(tokens[0], "seq", axis=0, tiled=True)
-    filt = lax.all_gather(long_filter.astype(BF16), "seq", axis=0, tiled=True).astype(F32)
+    n_dp, n_seq = lax.axis_size("dp"), lax.axis_size("seq")
+    filt, all_ids = gather_all(n_seq, long_filter.astype(BF16), tokens)
+    filt = filt.astype(F32)
     padded = jnp.pad(all_ids, (rim, rim), constant_values=4)
     ids_block = lax.dynamic_slice(padded, (block_start,), (block_len + 2 * rim,))
     layer_out, grad_mlp, grad_filter, small = compute(
         ids_block, tokens[0], table, q_own, embedding, gain_in, conv_taps, filt, gain_mid, mlp_weights, cotangent[0]
     )
-    small = lax.psum(small, ("dp", "seq"))
-    grad_emb, grad_gain, grad_conv, grad_mid = finish(small, embedding, gain_in, conv_taps)
-    mine = lax.psum_scatter(grad_filter.astype(BF16), "seq", scatter_dimension=0, tiled=True)
-    filter_out = lax.psum(mine, "dp").astype(F32)
-    cols = lax.psum_scatter(grad_mlp.astype(BF16), "seq", scatter_dimension=1, tiled=True).astype(F32)
-    mlp_out = lax.psum_scatter(cols, "dp", scatter_dimension=0, tiled=True)
+    mlp_out, filter_out, small = reduce_all(n_dp, n_seq, grad_mlp, grad_filter, small)
+    grad_emb, grad_gain, grad_conv, grad_mid = finish(small.T, embedding, gain_in, conv_taps)
     return layer_out[None], grad_emb, grad_gain, grad_conv, filter_out, grad_mid, mlp_out
 
 

time: 228 us -> 96.4 us (0.42)
  waiting for transfers between devices: 96.2 us -> 0 us
  blocking collectives: 60.8 us -> 0 us
  Pallas kernels: 0 us -> 52 us
  between operations: 14.2 us -> 1.15 us
  matrix products: 24.8 us -> 13.3 us
    pallas_call x0 -> x2, Pallas kernels: none -> 52 us  [the longest x1 36.4 us: reduce_all(): pl.pallas_call(lambda *refs: reduce_kernel(n_dp, n_seq, *refs), out_shape...]
    reduce_scatter x2 -> x0, waiting for transfers between devices: 49.2 us -> none  [the longest x1 38.6 us: on_device(): mlp_out = lax.psum_scatter(cols, 'dp', scatter_dimension=0, tiled=True)]
    psum x1 -> x0, blocking collectives: 39.8 us -> none  [on_device(): small = lax.psum(small, ('dp', 'seq'))]
    unnamed x5 -> x0, waiting for transfers between devices: 38.7 us -> none
    all_gather x2 -> x0, blocking collectives: 21 us -> none  [the longest x1 15.2 us: on_device(): lax.all_gather(long_filter.astype(BF16), 'seq', axis=0, tiled=True)]
    dot_general x17, matrix products: 24.8 us -> 13.3 us  [dot(): return lax.dot_general(a, b, (dims, ((), ())), preferred_element_type=F32)]
    psum x1 -> x0, waiting for transfers between devices: 8.27 us -> none  [on_device(): filter_out = lax.psum(mine, 'dp').astype(F32)]
    unnamed x65 -> x55, local copies, waits for them, and re-layouts: 9.33 us -> 7.3 us
  transfers between devices with their start and end apart: 4 -> 0, of which waited for: 4 -> 0; matrix products, arithmetic and copies ran while one was open for 13% -> 0% of each run, Pallas kernels for 0% -> 0%
where the time goes in v1:
time: 96.4 us; the launch traced here: 95.7 us
  Pallas kernels  52 us (54%)
  local copies, waits for them, and re-layouts  15.4 us (16%)
  other arithmetic  13.9 us (14%)
  matrix products  13.3 us (14%)
  between operations  1.15 us (1%)
    pallas_call x1, Pallas kernels, reduce_all(): pl.pallas_call(lambda *refs: reduce_kernel(n_dp, n_seq, *refs), out_shape...  36.4 us
    pallas_call x1, Pallas kernels, gather_all(): pl.pallas_call(lambda *refs: gather_kernel(n_seq, *refs), out_shape=(jax....  15.6 us
    dot_general x17, matrix products, dot(): return lax.dot_general(a, b, (dims, ((), ())), preferred_element_type=F32)  13.3 us
    unnamed x55, local copies, waits for them, and re-layouts  7.3 us
    rev x1, local copies, waits for them, and re-layouts, compute(): jnp.flip(combined[:, local_len:], 0)  2.2 us

profile of v1, /device:TPU:25, one launch (start us, length us, event | category | flops | bytes accessed | tf_op | source)
XLA Modules:
  0.0 95.7 jit_solution(17112936079244814873)
XLA Ops:
  0.7 1.0 multiply_reduce_fusion.6
  4.4 0.8 convert_bitcast_fusion.1
  5.1 0.9 slice_reduce_fusion.4
  6.0 0.7 multiply_convert_fusion.2
  6.7 1.7 %convert_element_type.92 = bf16[96,1024]{1,0:T(8,128)(2,1)} convert(f32[96,1024]{1,0:T(8,128)} %param.13) | non-fusion elementwise | flops 98304 | bytes 589824 | tf_op jit(solution)/shard_map/convert_element_type | solution.py:348
  8.4 1.0 %fusion.55 = (bf16[1,384,256]{2,1,0:T(8,128)(2,1)S(1)}, bf16[1,384,256]{2,1,0:T(8,128)(2,1)S(1)}) fusion(bf16[1,768,256]{2,1,0:T(8,128)(2,1)} %param.16), kind=kLoop, calls=%fused_computation.128 | loop fusion | bytes 786432 | tf_op jit(solution)/shard_map/slice | solution.py:60
  10.5 15.6 %gather.1 = (bf16[4,2,48,1024]{3,2,1,0:T(8,128)(2,1)}, s32[4,1,256]{2,1,0:T(1,128)}) custom-call(bf16[2,48,1024]{2,1,0:T(8,128)(2,1)} %bitcast.89, s32[1,256]{1,0:T(1,128)} %refs_1_.1), custom_call_target="tpu_custom_call" | custom-call | tf_op jit(solution)/shard_map/gather/pallas_call | solution.py:163
  26.1 1.0 %fusion.43 = (s32[1024]{0:T(1024)S(1)}, s32[1024]{0:T(1024)S(1)}, s32[1024]{0:T(1024)S(1)}, s32[1024]{0:T(1024)S(1)}, s32[1024]{0:T(1024)S(1)}, /*index=5*/s32[1024]{0:T(1024)S(1)}, s32[1024]{0:T(1024)S(1)}) fusion(s32[1024]{0:T(1024)} %bitcast.97), kind=kLoop, calls=%fused_computation.98 | loop fusion | flops 4096 | bytes 32768 | tf_op jit(solution)/shard_map/sub | solution.py:37
  27.1 0.8 iota_compare_fusion.6
  27.9 0.9 concatenate.51
  28.8 0.7 convolution_convert_fusion.5
  31.9 0.7 copy-done.7
  32.7 1.0 %convert_bitcast_fusion = f32[1536,512]{0,1:T(8,128)S(1)} fusion(bf16[2304,384]{1,0:T(8,128)(2,1)S(1)} %copy-done.7, f32[384,512]{0,1:T(8,128)S(1)} %get-tuple-element.44, f32[384]{0:T(512)S(1)} %copy-done.19, f32[512]{0:T(512)S(1)} %add_rsqrt_fusion), kind=kOutput, calls=%fused_computation | convolution fusion | flops 606142464 | bytes 5115904 | tf_op jit(solution)/shard_map/dot_general | solution.py:22
  33.7 2.2 %fusion.8 = (bf16[768,512]{0,1:T(8,128)(2,1)}, bf16[768,512]{0,1:T(8,128)(2,1)}, bf16[768,512]{0,1:T(8,128)(2,1)S(1)}) fusion(f32[1536,512]{0,1:T(8,128)S(1)} %convert_bitcast_fusion, bf16[2304,384]{1,0:T(8,128)(2,1)S(1)} %copy-done.7, bf16[384,256]{0,1:T(8,128)(2,1)S(1)} %rev.8, bf16[384,256]{0,1:T(8,128)(2,1)S(1)} %bitcast.90), kind=kOutput, calls=%fused_computation.21 | convolution fusion | flops 309067776 | bytes 6488064 | tf_op jit(solution)/shard_map/dot_general | solution.py:22
  36.6 1.4 %convolution_convert_fusion.4 = bf16[768,384]{1,0:T(8,128)(2,1)} fusion(bf16[768,512]{0,1:T(8,128)(2,1)S(1)} %get-tuple-element.47, bf16[384,256]{0,1:T(8,128)(2,1)S(1)} %rev.8, bf16[384,256]{0,1:T(8,128)(2,1)S(1)} %bitcast.91), kind=kOutput, calls=%fused_computation.28 | convolution fusion | flops 303071232 | bytes 1769472 | tf_op jit(solution)/shard_map/dot_general | solution.py:22
  38.0 0.7 fusion.56
  38.7 2.2 %rev.7 = bf16[384,256]{0,1:T(8,128)(2,1)} reverse(bf16[384,256]{0,1:T(8,128)(2,1)S(1)} %get-tuple-element.51), dimensions={0} | reverse | bytes 393216 | tf_op jit(solution)/shard_map/jit(_flip)/rev | solution.py:59
  40.9 1.8 %maximum_bitcast_fusion = bf16[1,768,256]{1,2,0:T(8,128)(2,1)} fusion(bf16[384,256]{0,1:T(8,128)(2,1)} %rev.7, bf16[384,256]{0,1:T(8,128)(2,1)} %get-tuple-element.50), kind=kLoop, calls=%fused_computation.59 | loop fusion | flops 786432 | bytes 786432 | tf_op jit(solution)/shard_map/broadcast_in_dim | solution.py:357
  42.7 1.9 %copy.26 = bf16[1,768,256]{2,1,0:T(8,128)(2,1)} copy(bf16[1,768,256]{1,2,0:T(8,128)(2,1)} %maximum_bitcast_fusion) | data formatting | bytes 786432
  44.6 2.6 %multiply_reduce_fusion = (f32[384]{0:T(512)S(1)}, f32[512]{0:T(512)S(1)}, f32[384,512]{0,1:T(8,128)S(1)}) fusion(f32[384,512]{0,1:T(8,128)S(1)} %get-tuple-element.44, f32[512]{0:T(512)S(1)} %add_rsqrt_fusion, f32[384]{0:T(512)} %param.14, bf16[2304,384]{1,0:T(8,128)(2,1)S(1)} %copy-done.8, bf16[768,512]{0,1:T(8,128)(2,1)} %get-tuple-element.46, ...), kind=kOutput, calls=%fused_computation.49 | convolution fusion | flops 608304256 | bytes 4332544 | tf_op jit(solution)/shard_map/dot_general | solution.py:22
  47.2 1.1 %convolution_convert_fusion.1 = bf16[1536,384]{1,0:T(8,128)(2,1)S(1)} fusion(bf16[768,512]{0,1:T(8,128)(2,1)S(1)} %copy-done.24, bf16[768,512]{0,1:T(8,128)(2,1)S(1)} %copy-done.23, f32[384,512]{0,1:T(8,128)S(1)} %get-tuple-element.44, f32[384]{0:T(512)S(1)} %copy-done.20, f32[512]{0:T(512)S(1)} %add_rsqrt_fusion), kind=kOutput, calls=%fused_computation.2 | convolution fusion | flops 608305152 | bytes 3542528 | tf_op jit(solution)/shard_map/dot_general | solution.py:22
  50.2 1.4 %copy-done.2 = bf16[1024,1024]{1,0:T(8,128)(2,1)S(1)} copy-done((bf16[1024,1024]{1,0:T(8,128)(2,1)S(1)}, bf16[1024,1024]{1,0:T(8,128)(2,1)}, u32[]{:S(2)}) %copy-start.2) | copy-done | bytes 2097176
  55.3 36.4 %reduce.11 = (f32[288,96]{1,0:T(8,128)S(1)}, f32[8,96,128]{2,1,0:T(8,128)S(1)}, f32[21,384]{1,0:T(8,128)S(1)}) custom-call(bf16[2,2,2,288,256]{4,3,2,1,0:T(8,128)(2,1)S(1)} %slice.130.refs_0_, bf16[2,2,2,288,128]{4,3,2,1,0:T(8,128)(2,1)S(1)} %slice.131.refs_1_, bf16[2,2,2,4,96,128]{5,4,3,2,1,0:T(8,128)(2,1)S(1)} %bitcast.77, ...), custom_call_target="tpu_custom_call" | custom-call | tf_op jit(solution)/shard_map/reduce/pallas_call | solution.py:305
  94.3 0.8 copy_bitcast_fusion
  (91 shorter events, 15.3 us)
Async XLA Ops:
  0.6 28.2 %copy-start.1 = (bf16[1024,1024]{1,0:T(8,128)(2,1)S(1)}, bf16[1024,1024]{1,0:T(8,128)(2,1)}, u32[]{:S(2)}) copy-start(bf16[1024,1024]{1,0:T(8,128)(2,1)} %constant.51.clone) | copy-start | bytes 6291460
  1.6 7.8 %copy-start.21 = (f32[4]{0:T(128)}, f32[4]{0:T(128)S(1)}, u32[]{:S(2)}) copy-start(f32[4]{0:T(128)S(1)} %add_rsqrt_fusion.1) | copy-start | bytes 52
  9.7 26.9 %copy-start.9 = (bf16[1,384,256]{1,2,0:T(8,128)(2,1)}, bf16[1,384,256]{1,2,0:T(8,128)(2,1)S(1)}, u32[]{:S(2)}) copy-start(bf16[1,384,256]{1,2,0:T(8,128)(2,1)S(1)} %copy.28) | copy-start | bytes 589828
  10.5 26.1 %copy-start.11 = (bf16[384,256]{0,1:T(8,128)(2,1)}, bf16[384,256]{0,1:T(8,128)(2,1)S(1)}, u32[]{:S(2)}) copy-start(bf16[384,256]{0,1:T(8,128)(2,1)S(1)} %rev.8) | copy-start | bytes 589828
  27.1 2.8 %copy-start = (bf16[4,2,48,1024]{3,2,1,0:T(8,128)(2,1)S(1)}, bf16[4,2,48,1024]{3,2,1,0:T(8,128)(2,1)}, u32[]{:S(2)}) copy-start(bf16[4,2,48,1024]{3,2,1,0:T(8,128)(2,1)} %get-tuple-element.12) | copy-start | bytes 2359300
  29.5 1.0 copy-start.13
  30.0 0.9 copy-start.3
  30.9 1.0 %copy-start.5 = (bf16[384,1024]{1,0:T(8,128)(2,1)}, bf16[384,1024]{1,0:T(8,128)(2,1)S(1)}, u32[]{:S(2)}) copy-start(bf16[384,1024]{1,0:T(8,128)(2,1)S(1)} %convolution_convert_fusion.3) | copy-start | bytes 2359300
  30.9 1.8 %copy-start.7 = (bf16[2304,384]{1,0:T(8,128)(2,1)S(1)}, bf16[2304,384]{1,0:T(8,128)(2,1)}, u32[]{:S(2)}) copy-start(bf16[2304,384]{1,0:T(8,128)(2,1)} %param.15) | copy-start | bytes 5308420
  30.9 1.8 %copy-start.19 = (f32[384]{0:T(512)S(1)}, f32[384]{0:T(512)}, u32[]{:S(2)}) copy-start(f32[384]{0:T(512)} %param.14) | copy-start | bytes 4612
  38.0 6.6 %copy-start.8 = (bf16[2304,384]{1,0:T(8,128)(2,1)S(1)}, bf16[2304,384]{1,0:T(8,128)(2,1)}, u32[]{:S(2)}) copy-start(bf16[2304,384]{1,0:T(8,128)(2,1)} %param.15) | copy-start | bytes 5308420
  44.6 2.6 %copy-start.20 = (f32[384]{0:T(512)S(1)}, f32[384]{0:T(512)}, u32[]{:S(2)}) copy-start(f32[384]{0:T(512)} %param.14) | copy-start | bytes 4612
  44.6 2.6 %copy-start.23 = (bf16[768,512]{0,1:T(8,128)(2,1)S(1)}, bf16[768,512]{0,1:T(8,128)(2,1)}, u32[]{:S(2)}) copy-start(bf16[768,512]{0,1:T(8,128)(2,1)} %get-tuple-element.45) | copy-start | bytes 2359300
  44.6 2.6 %copy-start.24 = (bf16[768,512]{0,1:T(8,128)(2,1)S(1)}, bf16[768,512]{0,1:T(8,128)(2,1)}, u32[]{:S(2)}) copy-start(bf16[768,512]{0,1:T(8,128)(2,1)} %get-tuple-element.46) | copy-start | bytes 2359300
  47.2 1.1 %copy-start.15 = (bf16[768,384]{1,0:T(8,128)(2,1)S(1)}, bf16[768,384]{1,0:T(8,128)(2,1)}, u32[]{:S(2)}) copy-start(bf16[768,384]{1,0:T(8,128)(2,1)} %convolution_convert_fusion.4) | copy-start | bytes 1769476
  48.3 0.9 copy-start.10
  48.3 1.0 %copy-start.12 = (bf16[384,256]{0,1:T(8,128)(2,1)S(1)}, bf16[384,256]{0,1:T(8,128)(2,1)}, u32[]{:S(2)}) copy-start(bf16[384,256]{0,1:T(8,128)(2,1)} %copy-done.11) | copy-start | bytes 589828
  50.0 1.6 %copy-start.2 = (bf16[1024,1024]{1,0:T(8,128)(2,1)S(1)}, bf16[1024,1024]{1,0:T(8,128)(2,1)}, u32[]{:S(2)}) copy-start(bf16[1024,1024]{1,0:T(8,128)(2,1)} %constant.51.clone) | copy-start | bytes 6291460
  52.0 1.1 %copy-start.4 = (bf16[384,1024]{1,0:T(8,128)(2,1)S(1)}, bf16[384,1024]{1,0:T(8,128)(2,1)}, u32[]{:S(2)}) copy-start(bf16[384,1024]{1,0:T(8,128)(2,1)} %copy-done.3) | copy-start | bytes 2359300
  52.0 1.4 %copy-start.6 = (bf16[384,1024]{1,0:T(8,128)(2,1)S(1)}, bf16[384,1024]{1,0:T(8,128)(2,1)}, u32[]{:S(2)}) copy-start(bf16[384,1024]{1,0:T(8,128)(2,1)} %copy-done.5) | copy-start | bytes 2359300
  55.2 37.1 %copy-start.17 = (f32[384,4]{0,1:T(4,128)S(1)}, f32[384,4]{0,1:T(4,128)}, u32[]{:S(2)}) copy-start(f32[384,4]{0,1:T(4,128)} %param.12) | copy-start | bytes 18436
  55.2 37.7 %copy-start.16 = (f32[4,384]{1,0:T(4,128)S(1)}, f32[4,384]{1,0:T(4,128)}, u32[]{:S(2)}) copy-start(f32[4,384]{1,0:T(4,128)} %param.10) | copy-start | bytes 18436
  55.2 37.7 %copy-start.18 = (f32[384]{0:T(512)S(1)}, f32[384]{0:T(512)}, u32[]{:S(2)}) copy-start(f32[384]{0:T(512)} %param.11) | copy-start | bytes 4612
  55.2 37.7 %copy-start.22 = (f32[4]{0:T(128)S(1)}, f32[4]{0:T(128)}, u32[]{:S(2)}) copy-start(f32[4]{0:T(128)} %copy-done.21) | copy-start | bytes 52
  (1 other events, 0.8 us)

commit v2 on v1

--- a/solution.py
+++ b/solution.py
@@ -22,83 +22,197 @@
     return lax.dot_general(a, b, (dims, ((), ())), preferred_element_type=F32)
 
 
-def compute(ids_block, ids_own, q_rows, q_own, embedding, gain_in, conv_taps, filt, gain_mid, mlp, cot):
-    taps = conv_taps.shape[1]
-    channels = embedding.shape[1]
-    block_len = q_rows.shape[0]
+def local_kernel(
+    n_seq, n_dp, tidy, all_ids, ids, table, emb_cols, gain_in, taps, filt, gain_mid, mlp, cot,
+    out, mlp_a, mlp_b, filt_out, small, full, spec_ref, level_ref, normed_ref, d_normed_ref, down_ref,
+):
+    channels, block_len = filt.shape[0] * filt.shape[1], filt.shape[2]
+    local_len = ids.shape[1]
     hidden = mlp.shape[0] // 3
-    local_len = ids_own.shape[0]
-    base_scale = lax.rsqrt(jnp.mean(embedding * embedding, axis=1, keepdims=True) + 1e-6)
-    base_norm = (embedding * base_scale * gain_in[None, :]).astype(BF16)
-    kmer = (conv_taps[:, :, None] * base_norm.astype(F32).T[:, None, :]).reshape(channels, -1).astype(BF16)
-    bases = jnp.arange(4, dtype=jnp.int32)[:, None]
-    rim = taps - 1
-    fwd = [ids_block[rim - k : rim - k + block_len] for k in range(taps)]
-    rev = [3 - ids_block[rim + k : rim + k + block_len] for k in range(taps)]
-    hot = jnp.concatenate([(row[None, :] == bases) for row in fwd + rev], 0).astype(BF16)
-    hot_spec = dot(hot, q_rows, ((1,), (1,))).astype(BF16)
-    half = 4 * taps
-    specs = [dot(kmer, hot_spec[s * half : (s + 1) * half], ((1,), (0,))).astype(BF16) for s in range(2)]
-    scaled = [(filt * spec.astype(F32)).astype(BF16) for spec in specs]
-    filtered = jnp.concatenate([dot(one, q_own, ((1,), (0,))) for one in scaled], 1)
-    both = jnp.concatenate([ids_own, 3 - ids_own])
-    emb_cols = embedding.T
-    residual = jnp.zeros((channels, 2 * local_len), F32)
+    n_taps = taps.shape[1]
+    half = 4 * n_taps
+    cut = mlp_a.shape[1]
+    place = lax.axis_index("seq")
+    per_block = block_len // local_len
+    first = place // per_block * per_block
+    last = first + per_block - 1
+    offset = pl.multiple_of((place - first) * local_len, local_len)
+    emb = emb_cols[...]
+    base_scale = lax.rsqrt(jnp.mean(emb * emb, axis=0, keepdims=True) + 1e-6)
+    base_norm = (emb * base_scale * gain_in[...]).astype(BF16).astype(F32)
+    lane = lax.broadcasted_iota(jnp.int32, (channels, half), 1)
+    tap_part = jnp.zeros((channels, half), F32)
+    base_part = jnp.zeros((channels, half), F32)
+    for k in range(n_taps):
+        tap_part = jnp.where(lane // 4 == k, taps[:, k : k + 1], tap_part)
     for a in range(4):
-        residual = residual + jnp.where(both[None, :] == a, emb_cols[:, a : a + 1], 0.0)
-    level = residual + filtered
+        base_part = jnp.where(lane % 4 == a, base_norm[:, a : a + 1], base_part)
+    kmer = (tap_part * base_part).astype(BF16)
+    edge = 128
+    before = jnp.where(first > 0, all_ids[jnp.maximum(first - 1, 0)][:, local_len - edge :], 4)
+    after = jnp.where(last < n_seq - 1, all_ids[jnp.minimum(last + 1, n_seq - 1)][:, :edge], 4)
+    row = jnp.concatenate([before] + [all_ids[first + j] for j in range(per_block)] + [after], 1)
+    width = block_len + 2 * edge
+    wide = jnp.broadcast_to(row, (8, width))
+    sub = lax.broadcasted_iota(jnp.int32, (8, block_len), 0)
+    tiles = []
+    for s in range(2):
+        for k in range(0, n_taps, 2):
+            shifts = [(k + i) if s == 0 else (width - k - i) % width for i in range(2)]
+            moved = [(pltpu.roll(wide, sh, 1) if sh else wide)[:, edge : edge + block_len] for sh in shifts]
+            picked = jnp.where(sub < 4, moved[0], moved[1])
+            want = sub % 4 if s == 0 else 3 - sub % 4
+            tiles.append(jnp.where(picked == want, 1.0, 0.0))
+    hot = jnp.concatenate(tiles, 0).astype(BF16)
+    hot_spec = dot(hot, table[...], ((1,), (0,))).astype(BF16)
+    rows = filt.shape[1]
+    for j in range(n_seq):
+        full[j * rows : (j + 1) * rows, :] = filt[j].astype(F32)
+    own = ids[...]
+    emb_all = emb_cols[...]
+    q_own = table[pl.ds(offset, local_len), :]
+    for s in range(2):
+        spec = dot(kmer, hot_spec[s * half : (s + 1) * half], ((1,), (0,))).astype(BF16)
+        spec_ref[s] = spec
+        scaled = (full[...] * spec.astype(F32)).astype(BF16)
+        mine = own if s == 0 else 3 - own
+        level = dot(scaled, q_own, ((1,), (1,)))
+        residual = jnp.zeros((channels, local_len), F32)
+        for a in range(4):
+            residual = jnp.where(mine == a, emb_all[:, a : a + 1], residual)
+        level_ref[:, s * local_len : (s + 1) * local_len] = level + residual
+    level = level_ref[...]
     mid_scale = lax.rsqrt(jnp.mean(level * level, axis=0, keepdims=True) + 1e-6)
+    normed_ref[...] = (level * mid_scale * gain_mid[...]).astype(BF16)
+    turn = jnp.where(
+        lax.broadcasted_iota(jnp.int32, (channels, channels), 0)
+        + lax.broadcasted_iota(jnp.int32, (channels, channels), 1)
+        == channels - 1,
+        1.0,
+        0.0,
+    ).astype(BF16)
+    turned = dot(turn, cot[channels:, :], ((1,), (0,))).astype(BF16)
+    back = jnp.concatenate([cot[:channels, :], turned], 1)
+    normed = normed_ref[...]
+    tile = 256 if hidden % 256 == 0 else hidden
+    for t in range(hidden // tile):
+        g0, u0, w0 = t * tile, hidden + t * tile, 2 * hidden + t * tile
+        w_gate, w_up, w_down = mlp[g0 : g0 + tile, :], mlp[u0 : u0 + tile, :], mlp[w0 : w0 + tile, :]
+        gate = dot(w_gate, normed, ((1,), (0,)))
+        up = dot(w_up, normed, ((1,), (0,)))
+        d_act = dot(w_down, back, ((1,), (0,)))
+        sig = jax.nn.sigmoid(gate)
+        silu = gate * sig
+        act = (silu * up).astype(BF16)
+        d_gate = (d_act * up * (sig + silu * (1.0 - sig))).astype(BF16)
+        d_up = (d_act * silu).astype(BF16)
+        down = dot(w_down, act, ((0,), (0,)))
+        down_ref[...] = down if t == 0 else down_ref[...] + down
+        d_part = dot(w_gate, d_gate, ((0,), (0,))) + dot(w_up, d_up, ((0,), (0,)))
+        d_normed_ref[...] = d_part if t == 0 else d_normed_ref[...] + d_part
+        for start, left, right in ((g0, d_gate, normed), (u0, d_up, normed), (w0, act, back)):
+            grad = dot(left, right, ((1,), (1,))).astype(BF16)
+            mlp_a[start : start + tile, :] = grad[:, :cut]
+            mlp_b[start : start + tile, :] = grad[:, cut:]
+    combined = (level_ref[...] + down_ref[...]).astype(BF16)
+    out[:channels, :] = combined[:, :local_len]
+    out[channels:, :] = dot(turn, combined[:, local_len:], ((1,), (0,))).astype(BF16)
     unit = level * mid_scale
-    normed = (unit * gain_mid[:, None]).astype(BF16)
-    w_in, w_down = mlp[: 2 * hidden], mlp[2 * hidden :]
-    proj = dot(w_in, normed, ((1,), (0,))).astype(BF16).astype(F32)
-    gate, up = proj[:hidden], proj[hidden:]
-    sig = jax.nn.sigmoid(gate)
-    act = (gate * sig * up).astype(BF16)
-    combined = (level + dot(w_down, act, ((0,), (0,)))).astype(BF16)
-    layer_out = jnp.concatenate([combined[:, :local_len], jnp.flip(combined[:, local_len:], 0)], 0)
-    back = jnp.concatenate([cot[:channels], jnp.flip(cot[channels:], 0)], 1)
-    d_act = dot(w_down, back, ((1,), (0,)))
-    d_gate = d_act * up * sig * (1.0 + gate * (1.0 - sig))
-    d_up = d_act * gate * sig
-    d_proj = jnp.concatenate([d_gate, d_up], 0).astype(BF16)
-    d_normed = dot(w_in, d_proj, ((0,), (0,)))
-    grad_in = dot(d_proj, normed, ((1,), (1,)))
-    grad_down = dot(act, back, ((1,), (1,)))
-    grad_mlp = jnp.concatenate([grad_in, grad_down], 0)
-    grad_mid = jnp.sum(d_normed * unit, axis=1, keepdims=True)
-    d_unit = d_normed * gain_mid[:, None]
+    d_normed = d_normed_ref[...]
+    mid_grad = d_normed * unit
+    d_unit = d_normed * gain_mid[...]
     d_level = back.astype(F32) + mid_scale * (d_unit - unit * jnp.mean(d_unit * unit, axis=0, keepdims=True))
     d_bf = d_level.astype(BF16)
-    own_hot = (both[None, :] == bases).astype(BF16)
     d_low = (d_level - d_bf.astype(F32)).astype(BF16)
-    base_sum = dot(d_bf, own_hot, ((1,), (1,))) + dot(d_low, own_hot, ((1,), (1,)))
-    grad_filter = jnp.zeros(filt.shape, F32)
-    kmer_sum = jnp.zeros((channels, half), F32)
+    both = jnp.concatenate([own, 3 - own], 1)
+    sub8 = lax.broadcasted_iota(jnp.int32, (8, 2 * local_len), 0)
+    own_hot = jnp.where(sub8 == both, 1.0, 0.0).astype(BF16)
+    ones = jnp.ones((8, 2 * local_len), BF16)
+    m_bf = mid_grad.astype(BF16)
+    m_low = (mid_grad - m_bf.astype(F32)).astype(BF16)
+    small[half : half + 8, :] = dot(own_hot, d_bf, ((1,), (1,))) + dot(own_hot, d_low, ((1,), (1,)))
+    small[half + 8 : half + 16, :] = dot(ones, m_bf, ((1,), (1,))) + dot(ones, m_low, ((1,), (1,)))
+    q_rows = table[pl.ds(offset, local_len), :]
+    grad_filter = jnp.zeros((channels, block_len), F32)
+    kmer_sum = jnp.zeros((half, channels), F32)
     for s in range(2):
-        d_scaled = dot(d_bf[:, s * local_len : (s + 1) * local_len], q_own, ((1,), (1,)))
-        grad_filter = grad_filter + d_scaled * specs[s].astype(F32)
-        d_spec = (filt * d_scaled).astype(BF16)
-        kmer_sum = kmer_sum + dot(d_spec, hot_spec[s * half : (s + 1) * half], ((1,), (1,)))
-    small = jnp.concatenate([base_sum, kmer_sum, grad_mid], 1).T
-    return layer_out, grad_mlp, grad_filter, small
+        d_scaled = dot(d_bf[:, s * local_len : (s + 1) * local_len], q_rows, ((1,), (0,)))
+        grad_filter = grad_filter + d_scaled * spec_ref[s].astype(F32)
+        d_spec = (full[...] * d_scaled).astype(BF16)
+        kmer_sum = kmer_sum + dot(hot_spec[s * half : (s + 1) * half], d_spec, ((1,), (1,)))
+    small[:half, :] = kmer_sum
+    grad_filter = grad_filter.astype(BF16)
+    if tidy:
+        piece = block_len // n_dp
+        for i in range(n_dp):
+            filt_out[i] = grad_filter[:, i * piece : (i + 1) * piece]
+    else:
+        filt_out[...] = grad_filter
+
+
+def compute(n_seq, n_dp, all_ids, ids, embedding, gain_in, conv_taps, filt, gain_mid, mlp, cot):
+    channels = embedding.shape[1]
+    block_len = filt.shape[-1]
+    local_len = ids.shape[1]
+    table = jnp.asarray(dct_table(block_len).T)
+    cut = channels // 128 * 2 // 3 * 128
+    tidy = block_len % (n_dp * 128) == 0
+    f_shape = (n_dp, channels, block_len // n_dp) if tidy else (channels, block_len)
+    sums = 4 * conv_taps.shape[1] + 16
+    vmem = pl.BlockSpec(memory_space=pltpu.VMEM)
+    return pl.pallas_call(
+        lambda *refs: local_kernel(n_seq, n_dp, tidy, *refs),
+        out_shape=(
+            jax.ShapeDtypeStruct(cot.shape, BF16),
+            jax.ShapeDtypeStruct((mlp.shape[0], cut), BF16),
+            jax.ShapeDtypeStruct((mlp.shape[0], channels - cut), BF16),
+            jax.ShapeDtypeStruct(f_shape, BF16),
+            jax.ShapeDtypeStruct((sums, channels), F32),
+        ),
+        in_specs=[vmem] * 10,
+        out_specs=[vmem] * 5,
+        scratch_shapes=[
+            pltpu.VMEM((channels, block_len), F32),
+            pltpu.VMEM((2, channels, block_len), BF16),
+            pltpu.VMEM((channels, 2 * local_len), F32),
+            pltpu.VMEM((channels, 2 * local_len), BF16),
+            pltpu.VMEM((channels, 2 * local_len), F32),
+            pltpu.VMEM((channels, 2 * local_len), F32),
+        ],
+        compiler_params=pltpu.CompilerParams(vmem_limit_bytes=58 * 2**20),
+        name="local",
+    )(all_ids, ids, table, embedding.T, gain_in[:, None], conv_taps, filt, gain_mid[:, None], mlp, cot)
+
+
+def finish_kernel(small, embedding, gain_in, taps, grad_emb, grad_gain, grad_conv, grad_mid):
+    n_taps = taps.shape[0]
+    emb = embedding[...]
+    base_scale = lax.rsqrt(jnp.mean(emb * emb, axis=1, keepdims=True) + 1e-6)
+    unit = emb * base_scale
+    base_norm = (unit * gain_in[...]).astype(BF16).astype(F32)
+    d_norm = jnp.zeros(emb.shape, F32)
+    for k in range(n_taps):
+        part = small[4 * k : 4 * k + 4, :]
+        d_norm = d_norm + part * taps[k : k + 1, :]
+        grad_conv[k : k + 1, :] = jnp.sum(part * base_norm, axis=0, keepdims=True)
+    grad_gain[...] = jnp.sum(d_norm * unit, axis=0, keepdims=True)
+    d_unit = d_norm * gain_in[...]
+    base_sum = small[4 * n_taps : 4 * n_taps + 4, :]
+    grad_emb[...] = base_sum + base_scale * (d_unit - unit * jnp.mean(d_unit * unit, axis=1, keepdims=True))
+    grad_mid[...] = small[4 * n_taps + 8 : 4 * n_taps + 9, :]
 
 
 def finish(small, embedding, gain_in, conv_taps):
-    taps = conv_taps.shape[1]
-    channels = embedding.shape[1]
-    base_sum = small[:, :4].T
-    kmer_sum = small[:, 4 : 4 + 4 * taps].reshape(channels, taps, 4)
-    grad_mid = small[:, 4 + 4 * taps]
-    base_scale = lax.rsqrt(jnp.mean(embedding * embedding, axis=1, keepdims=True) + 1e-6)
-    unit = embedding * base_scale
-    base_norm = (unit * gain_in[None, :]).astype(BF16).astype(F32)
-    grad_conv = jnp.sum(kmer_sum * base_norm.T[:, None, :], axis=2)
-    d_norm = jnp.sum(kmer_sum * conv_taps[:, :, None], axis=1).T
-    grad_gain = jnp.sum(d_norm * unit, axis=0)
-    d_unit = d_norm * gain_in[None, :]
-    grad_emb = base_sum + base_scale * (d_unit - unit * jnp.mean(d_unit * unit, axis=1, keepdims=True))
-    return grad_emb, grad_gain, grad_conv, grad_mid
+    row = jax.ShapeDtypeStruct((1, embedding.shape[1]), F32)
+    vmem = pl.BlockSpec(memory_space=pltpu.VMEM)
+    grad_emb, grad_gain, grad_conv, grad_mid = pl.pallas_call(
+        finish_kernel,
+        out_shape=(jax.ShapeDtypeStruct(embedding.shape, F32), row, jax.ShapeDtypeStruct(conv_taps.shape[::-1], F32), row),
+        in_specs=[vmem] * 4,
+        out_specs=[vmem] * 4,
+        name="finish",
+    )(small, embedding, gain_in[None, :], conv_taps.T)
+    return grad_emb, grad_gain[0], grad_conv.T, grad_mid[0]
 
 
 MESH = pl.DeviceIdType.MESH
@@ -128,26 +242,30 @@
     core = lax.rem(dp, 2)
     mate = (dp + 1 - 2 * core, sq)
     peers = ring_of(sq, n_seq, lambda j: (dp, j))
+    gath[sq] = shard[...].astype(BF16)
+    wide = shard.shape[1] // 2
+    low = pl.multiple_of(core * wide, wide)
+    high = pl.multiple_of((1 - core) * wide, wide)
     greet([mate], peers)
     sends = []
     for off in range(1, n_seq):
         id_copy = remote(ids, all_ids.at[sq], id_send.at[off], id_recv.at[off], peers[off - 1])
-        copy = remote(shard.at[core], gath.at[sq, core], send.at[off], recv.at[off], peers[off - 1])
+        part = gath.at[sq, :, pl.ds(low, wide)]
+        copy = remote(part, part, send.at[off], recv.at[off], peers[off - 1])
         id_copy.start()
         copy.start()
         sends += [id_copy, copy]
     all_ids[sq] = ids[...]
-    gath[sq] = shard[...]
     for off in [*range(n_seq - 1, 0, -1)]:
         source = lax.rem(sq - off + n_seq, n_seq)
-        landed = gath.at[source, core]
+        landed = gath.at[source, :, pl.ds(low, wide)]
         remote(landed, landed, send.at[off], recv.at[off], mate).wait_recv()
         swap = remote(landed, landed, swap_send.at[off], swap_recv.at[off], mate)
         swap.start()
         sends.append(swap)
     for off in range(1, n_seq):
         source = lax.rem(sq - off + n_seq, n_seq)
-        other = gath.at[source, 1 - core]
+        other = gath.at[source, :, pl.ds(high, wide)]
         remote(other, other, swap_send.at[off], swap_recv.at[off], mate).wait_recv()
         got = all_ids.at[source]
         remote(got, got, id_send.at[off], id_recv.at[off], mate).wait_recv()
@@ -157,13 +275,12 @@
 
 def gather_all(n_seq, shard, ids):
     rows, width = shard.shape
-    halves = shard.reshape(2, rows // 2, width)
     vmem = pl.BlockSpec(memory_space=pltpu.VMEM)
     dma = pltpu.SemaphoreType.DMA((n_seq,))
     gath, all_ids = pl.pallas_call(
         lambda *refs: gather_kernel(n_seq, *refs),
         out_shape=(
-            jax.ShapeDtypeStruct((n_seq,) + halves.shape, shard.dtype),
+            jax.ShapeDtypeStruct((n_seq, rows, width), BF16),
             jax.ShapeDtypeStruct((n_seq,) + ids.shape, ids.dtype),
         ),
         in_specs=[vmem] * 2,
@@ -171,8 +288,8 @@
         scratch_shapes=[dma] * 6,
         compiler_params=pltpu.CompilerParams(collective_id=0, has_side_effects=True),
         name="gather",
-    )(halves, ids)
-    return gath.reshape(n_seq * rows, width), all_ids.reshape(-1)
+    )(shard, ids)
+    return gath, all_ids
 
 
 def at_axis(axis, index):
@@ -274,21 +391,21 @@
         copy.wait_send()
 
 
-def reduce_all(n_dp, n_seq, grad_mlp, grad_filter, small):
+def reduce_all(n_dp, n_seq, mlp_a, mlp_b, filt, small):
     bits = n_dp.bit_length() - 1
     twos = (2,) * bits
-    rows, width = grad_mlp.shape
+    lanes = 128
+    rows, cut = mlp_a.shape
+    width = cut + mlp_b.shape[1]
     part = rows // n_dp
-    lanes = 128
-    cut = width // lanes * 2 // 3 * lanes
-    mlp = grad_mlp.astype(BF16).reshape(twos + (part, width))
-    mlp_a, mlp_b = mlp[..., :cut], mlp[..., cut:]
-    chan, length = grad_filter.shape
+    mlp_a = mlp_a.reshape(twos + (part, cut))
+    mlp_b = mlp_b.reshape(twos + (part, width - cut))
+    tidy = filt.ndim == 3
+    chan = filt.shape[-2]
+    length = filt.shape[-1] * (n_dp if tidy else 1)
     own = chan // n_seq
-    tidy = length % (n_dp * lanes) == 0
-    filt = grad_filter.astype(BF16)
     if tidy:
-        filt = filt.reshape(n_seq, own, n_dp, length // n_dp).transpose(2, 0, 1, 3)
+        filt = filt.reshape(n_dp, n_seq, own, length // n_dp)
     else:
         filt = filt.reshape(n_seq, n_dp, -1, lanes).transpose(1, 0, 2, 3)
     f_tail = filt.shape[1:]
@@ -337,23 +454,13 @@
 
 
 def on_device(tokens, embedding, gain_in, conv_taps, long_filter, gain_mid, mlp_weights, cotangent):
-    local_len = tokens.shape[1]
-    block_len = long_filter.shape[1]
-    rim = conv_taps.shape[1] - 1
-    place = lax.axis_index("seq") * local_len
-    block_start = place // block_len * block_len
-    table = jnp.asarray(dct_table(block_len))
-    q_own = lax.dynamic_slice(table, (0, place - block_start), (block_len, local_len))
     n_dp, n_seq = lax.axis_size("dp"), lax.axis_size("seq")
-    filt, all_ids = gather_all(n_seq, long_filter.astype(BF16), tokens)
-    filt = filt.astype(F32)
-    padded = jnp.pad(all_ids, (rim, rim), constant_values=4)
-    ids_block = lax.dynamic_slice(padded, (block_start,), (block_len + 2 * rim,))
-    layer_out, grad_mlp, grad_filter, small = compute(
-        ids_block, tokens[0], table, q_own, embedding, gain_in, conv_taps, filt, gain_mid, mlp_weights, cotangent[0]
+    filt, all_ids = gather_all(n_seq, long_filter, tokens)
+    layer_out, mlp_a, mlp_b, grad_filter, small = compute(
+        n_seq, n_dp, all_ids, tokens, embedding, gain_in, conv_taps, filt, gain_mid, mlp_weights, cotangent[0]
     )
-    mlp_out, filter_out, small = reduce_all(n_dp, n_seq, grad_mlp, grad_filter, small)
-    grad_emb, grad_gain, grad_conv, grad_mid = finish(small.T, embedding, gain_in, conv_taps)
+    mlp_out, filter_out, small = reduce_all(n_dp, n_seq, mlp_a, mlp_b, grad_filter, small)
+    grad_emb, grad_gain, grad_conv, grad_mid = finish(small, embedding, gain_in, conv_taps)
     return layer_out[None], grad_emb, grad_gain, grad_conv, filter_out, grad_mid, mlp_out
 
 

time: 96.4 us -> 81.6 us (0.85)
  matrix products: 13.3 us -> 0 us
  Pallas kernels: 52 us -> 65 us
  other arithmetic: 13.9 us -> 2.53 us
  local copies, waits for them, and re-layouts: 15.4 us -> 12.9 us
    dot_general x17 -> x0, matrix products: 13.3 us -> none  [dot(): return lax.dot_general(a, b, (dims, ((), ())), preferred_element_type=F32)]
    pallas_call x0 -> x2, Pallas kernels: none -> 11.9 us  [the longest x1 10.3 us: compute(): pl.pallas_call(lambda *refs: local_kernel(n_seq, n_dp, tidy, *refs), out_...]
    broadcast_in_dim x1 -> x3, local copies, waits for them, and re-layouts: 0.01 us -> 3.51 us  [the longest x1 1.48 us: compute(): gain_in[:, None]]
    slice x7 -> x0, local copies, waits for them, and re-layouts: 3.42 us -> none  [the longest x1 1.05 us: compute(): back = jnp.concatenate([cot[:channels], jnp.flip(cot[channels:], 0)], 1)]
    rev x2 -> x0, local copies, waits for them, and re-layouts: 2.84 us -> none  [the longest x1 2.2 us: compute(): jnp.flip(combined[:, local_len:], 0)]
    reduce_sum x4 -> x0, other arithmetic: 2.69 us -> none  [the longest x1 0.95 us: compute(): jnp.mean(embedding * embedding, axis=1, keepdims=True) + 1e-06]
    convert_element_type x3 -> x0, other arithmetic: 2.65 us -> none  [the longest x1 1.7 us: on_device(): filt, all_ids = gather_all(n_seq, long_filter.astype(BF16), tokens)]
    pallas_call x0 -> x2, other arithmetic: none -> 2.53 us  [finish(): pl.pallas_call(finish_kernel, out_shape=(jax.ShapeDtypeStruct(embedding.s...]
where the time goes in v2:
time: 81.6 us; the launch traced here: 81 us
  Pallas kernels  65 us (80%)
  local copies, waits for them, and re-layouts  12.9 us (16%)
  other arithmetic  2.53 us (3%)
    pallas_call x1, Pallas kernels, reduce_all(): pl.pallas_call(lambda *refs: reduce_kernel(n_dp, n_seq, *refs), out_shape...  37.5 us
    pallas_call x1, Pallas kernels, gather_all(): pl.pallas_call(lambda *refs: gather_kernel(n_seq, *refs), out_shape=(jax....  15.7 us
    pallas_call x1, Pallas kernels, compute(): pl.pallas_call(lambda *refs: local_kernel(n_seq, n_dp, tidy, *refs), out_...  10.3 us
    unnamed x15, local copies, waits for them, and re-layouts  8.57 us
    pallas_call x2, other arithmetic, finish(): pl.pallas_call(finish_kernel, out_shape=(jax.ShapeDtypeStruct(embedding.s...  2.53 us

profile of v2, /device:TPU:25, one launch (start us, length us, event | category | flops | bytes accessed | tf_op | source)
XLA Modules:
  0.0 81.0 jit_solution(6594375190406186886)
XLA Ops:
  0.6 15.7 %gather.1 = (bf16[4,96,1024]{2,1,0:T(8,128)(2,1)}, s32[4,1,256]{2,1,0:T(1,128)}) custom-call(f32[96,1024]{1,0:T(8,128)} %refs_0_.1, s32[1,256]{1,0:T(1,128)} %refs_1_.3), custom_call_target="tpu_custom_call" | custom-call | tf_op jit(solution)/shard_map/gather/pallas_call | solution.py:280
  16.3 1.5 %copy.18 = f32[4,384]{0,1:T(8,128)} copy(f32[4,384]{1,0:T(4,128)} %embedding.1) | data formatting | bytes 12288 | tf_op args[1]
  17.8 1.5 %broadcast_in_dim.16.refs_4_ = f32[384,1]{1,0:T(8,128)} reshape(f32[384]{0:T(512)} %param.11) | data formatting | bytes 3072 | tf_op jit(solution)/shard_map/broadcast_in_dim | solution.py:184
  19.3 1.5 %broadcast_in_dim.17.refs_7_ = f32[384,1]{1,0:T(8,128)} reshape(f32[384]{0:T(512)} %param.14) | data formatting | bytes 3072 | tf_op jit(solution)/shard_map/broadcast_in_dim | solution.py:184
  20.8 1.5 %copy.20.refs_5_ = f32[384,4]{1,0:T(8,128)} copy(f32[384,4]{0,1:T(4,128)} %param.12) | data formatting | bytes 12288 | tf_op args[3]
  22.3 10.3 %local.1 = (bf16[768,256]{1,0:T(8,128)(2,1)}, bf16[2304,256]{1,0:T(8,128)(2,1)}, bf16[2304,128]{1,0:T(8,128)(2,1)}, bf16[8,384,128]{2,1,0:T(8,128)(2,1)}, f32[32,384]{1,0:T(8,128)}) custom-call(s32[4,1,256]{2,1,0:T(1,128)} %get-tuple-element.21.refs_0_, s32[1,256]{1,0:T(1,128)} %refs_1_.3, bf16[1024,1024]{1,0:T(8,128)(2,1)} %constant.2.clone.refs_2_, ...), custom_call_target="tpu_custom_call" | custom-call | tf_op jit(solution)/shard_map/local/pallas_call | solution.py:163
  32.5 0.0 copy-start.5
  32.5 0.0 copy-start
  32.5 1.3 %copy-done = bf16[2304,256]{1,0:T(8,128)(2,1)S(1)} copy-done((bf16[2304,256]{1,0:T(8,128)(2,1)S(1)}, bf16[2304,256]{1,0:T(8,128)(2,1)}, u32[]{:S(2)}) %copy-start) | copy-done | bytes 1179672
  33.8 1.1 %copy-done.1 = bf16[8,384,128]{2,1,0:T(8,128)(2,1)S(1)} copy-done((bf16[8,384,128]{2,1,0:T(8,128)(2,1)S(1)}, bf16[8,384,128]{2,1,0:T(8,128)(2,1)}, u32[]{:S(2)}) %copy-start.1) | copy-done | bytes 786456
  35.0 0.0 copy-start.2
  35.0 1.1 %copy-done.2 = bf16[2304,128]{1,0:T(8,128)(2,1)S(1)} copy-done((bf16[2304,128]{1,0:T(8,128)(2,1)S(1)}, bf16[2304,128]{1,0:T(8,128)(2,1)}, u32[]{:S(2)}) %copy-start.2) | copy-done | bytes 589848
  36.0 0.0 copy-start.4
  36.0 0.8 copy-done.4
  36.8 37.5 %reduce.3 = (f32[288,96]{1,0:T(8,128)S(1)}, f32[8,96,128]{2,1,0:T(8,128)S(1)}, f32[32,384]{1,0:T(8,128)S(1)}) custom-call(bf16[2,2,2,288,256]{4,3,2,1,0:T(8,128)(2,1)S(1)} %bitcast.14, bf16[2,2,2,288,128]{4,3,2,1,0:T(8,128)(2,1)S(1)} %bitcast.16, bf16[2,2,2,4,96,128]{5,4,3,2,1,0:T(8,128)(2,1)S(1)} %bitcast.15, f32[32,384]{1,0:T(8,128)S(1)} %copy-done.4), custom_call_target="tpu_custom_call" | custom-call | tf_op jit(solution)/shard_map/reduce/pallas_call | solution.py:422
  74.3 0.0 copy-start.3
  74.3 0.6 copy-done.3
  74.9 0.0 copy-done.5
  74.9 0.6 broadcast_in_dim.15.gain_in
  75.5 1.6 %finish.1 = (f32[4,384]{1,0:T(4,128)}, f32[1,384]{1,0:T(1,128)}, f32[4,384]{1,0:T(4,128)}, f32[1,384]{1,0:T(1,128)}) custom-call(f32[32,384]{1,0:T(8,128)} %copy-done.3, f32[4,384]{1,0:T(4,128)} %embedding.1, f32[1,384]{1,0:T(1,128)} %broadcast_in_dim.15.gain_in, f32[4,384]{1,0:T(4,128)} %bitcast.19), custom_call_target="tpu_custom_call" | custom-call | tf_op jit(solution)/shard_map/finish/pallas_call | solution.py:208
  77.1 1.3 %reduce.1 = f32[384]{0:T(512)} reduce(f32[1,384]{1,0:T(1,128)} %get-tuple-element.30, f32[]{:T(128)} %constant.5), dimensions={0}, to_apply=%get-tuple-element.30.reduce_sub_computation | reduce | bytes 3076 | tf_op jit(solution)/shard_map/finish/pallas_call | solution.py:208
  78.3 1.3 %reduce.2 = f32[384]{0:T(512)} reduce(f32[1,384]{1,0:T(1,128)} %get-tuple-element.33, f32[]{:T(128)} %constant.5), dimensions={0}, to_apply=%get-tuple-element.33.reduce_sub_computation | reduce | bytes 3076 | tf_op jit(solution)/shard_map/finish/pallas_call | solution.py:208
  79.6 0.8 copy_bitcast_fusion
  80.4 0.7 copy.26
  (1 shorter events, 0.0 us)
Async XLA Ops:
  32.5 42.4 %copy-start.5 = (f32[384]{0:T(512)S(1)}, f32[384]{0:T(512)}, u32[]{:S(2)}) copy-start(f32[384]{0:T(512)} %param.11) | copy-start | bytes 4612
  32.5 1.3 %copy-start = (bf16[2304,256]{1,0:T(8,128)(2,1)S(1)}, bf16[2304,256]{1,0:T(8,128)(2,1)}, u32[]{:S(2)}) copy-start(bf16[2304,256]{1,0:T(8,128)(2,1)} %get-tuple-element.24) | copy-start | bytes 3538948
  33.8 1.1 %copy-start.1 = (bf16[8,384,128]{2,1,0:T(8,128)(2,1)S(1)}, bf16[8,384,128]{2,1,0:T(8,128)(2,1)}, u32[]{:S(2)}) copy-start(bf16[8,384,128]{2,1,0:T(8,128)(2,1)} %get-tuple-element.26) | copy-start | bytes 2359300
  35.0 1.1 %copy-start.2 = (bf16[2304,128]{1,0:T(8,128)(2,1)S(1)}, bf16[2304,128]{1,0:T(8,128)(2,1)}, u32[]{:S(2)}) copy-start(bf16[2304,128]{1,0:T(8,128)(2,1)} %get-tuple-element.25) | copy-start | bytes 1769476
  36.0 0.8 copy-start.4
  74.3 0.6 copy-start.3
